TPU v7x, 32 devices: a whole 2x2x4 slice. The times are simulated.
32 devices in a mesh: dp: 16 (over z, y, x), grp: 2 (over core).
Axes of the slice: x: 2, y: 2, z: 4, core: 2. Of those that a mesh axis runs over, the one named last changes fastest.
Arguments:
- query_features: bfloat16 [32768, 512], P(('dp', 'grp')), may hold values from -256 to 256
- query_weights: bfloat16 [32768], P(('dp', 'grp')), may hold values from 0.5 to 13.5, as said below
- positive_index: int32 [32768], P(('dp', 'grp')), may hold values from 0 to 511
- item_features: bfloat16 [512, 512], P(('dp', 'grp')), may hold values from -6 to 6
- item_ids: int32 [512], P(('dp', 'grp')), may hold values from 0 to 255
- item_logq: bfloat16 [512], P(('dp', 'grp')), may hold values from -14 to -11
- query_w_in: bfloat16 [512, 1024], replicated, may hold values from -0.25 to 0.25
- query_w_out: bfloat16 [1024, 256], replicated, may hold values from -0.1875 to 0.1875
- item_w_in: bfloat16 [512, 1024], replicated, may hold values from -0.25 to 0.25
- item_w_out: bfloat16 [1024, 256], replicated, may hold values from -0.1875 to 0.1875
Outputs:
- grad_query_w_in: float32 [512, 1024], replicated
- grad_query_w_out: float32 [1024, 256], replicated
- grad_item_w_in: float32 [512, 1024], replicated
- grad_item_w_out: float32 [1024, 256], replicated
Inputs may be any that keep to these rules, and one draw needn't show every extreme that they name: `query_weights`: positive weights. `item_ids`: an id may occur several times in the sample set.
All inputs are finite; a program needn't handle non-finite values.
Results may differ from a plain program's by a relative error of at most 0.013.
Values may be sent and summed in bfloat16 or wider, within the bound.
A program may use at most 128 MiB of HBM per device.

v0:
```python
import jax
import jax.numpy as jnp
from jax import lax
from jax.sharding import PartitionSpec as P

score_scale = 0.25
loss_scale = 1024.0


def silu_slope(values):
    gate = jax.nn.sigmoid(values)
    return gate * (1.0 + values * (1.0 - gate))


def tower(features, weight_in, weight_out):
    pre_act = jnp.dot(features, weight_in, preferred_element_type=jnp.float32)
    hidden = jax.nn.silu(pre_act).astype(jnp.bfloat16)
    embedding = jnp.dot(hidden, weight_out, preferred_element_type=jnp.float32).astype(jnp.bfloat16)
    return (pre_act, hidden, embedding)


def tower_back(features, pre_act, hidden, weight_out, embed_grad):
    grad_out = jnp.dot(hidden.T, embed_grad, preferred_element_type=jnp.float32)
    hidden_grad = jnp.dot(embed_grad, weight_out.T, preferred_element_type=jnp.float32)
    pre_grad = (hidden_grad * silu_slope(pre_act)).astype(jnp.bfloat16)
    grad_in = jnp.dot(features.T, pre_grad, preferred_element_type=jnp.float32)
    return (grad_in, grad_out)


def item_scores(query_rows, items, item_bias, item_codes, columns, positives, pos_codes):
    raw_scores = lax.dot_general(
        query_rows, items, (((1,), (1,)), ((), ())), preferred_element_type=jnp.float32
    )
    scores = score_scale * raw_scores - item_bias.astype(jnp.float32)[None, :]
    masked_hits = (item_codes[None, :] == pos_codes[:, None]) & (
        columns[None, :] != positives[:, None]
    )
    return jnp.where(masked_hits, -jnp.inf, scores)


def partial_stats(scores):
    row_max = jnp.maximum(jnp.max(scores, axis=1), -1e30)
    row_sum = jnp.sum(jnp.exp(scores - row_max[:, None]), axis=1)
    return (row_max, row_sum)


def finish(scores, row_max, row_sum, columns, positives, weights):
    probability = jnp.exp(scores - row_max[:, None]) / row_sum[:, None]
    target = (columns[None, :] == positives[:, None]).astype(jnp.float32)
    return (weights.astype(jnp.float32)[:, None] * (probability - target)).astype(jnp.bfloat16)


def positive_codes(every_code, positives):
    slots = jnp.arange(every_code.shape[0], dtype=jnp.int32)
    return jnp.sum(jnp.where(positives[:, None] == slots[None, :], every_code[None, :], 0), axis=1)


def on_device(
    query_features,
    query_weights,
    positive_index,
    item_features,
    item_ids,
    item_logq,
    query_w_in,
    query_w_out,
    item_w_in,
    item_w_out,
):
    weight_part = jnp.sum(query_weights.astype(jnp.float32))
    weight_total = lax.psum(weight_part, ("dp", "grp"))
    query_pre, query_hidden, query_embed = tower(query_features, query_w_in, query_w_out)
    item_pre, item_hidden, item_embed = tower(item_features, item_w_in, item_w_out)
    items_all, bias_all, codes_all = (
        lax.all_gather(item_embed, ("dp", "grp"), axis=0, tiled=True),
        lax.all_gather(item_logq, ("dp", "grp"), axis=0, tiled=True),
        lax.all_gather(item_ids, ("dp", "grp"), axis=0, tiled=True),
    )
    columns = jnp.arange(items_all.shape[0], dtype=jnp.int32)
    pos_codes = positive_codes(codes_all, positive_index)
    scores = item_scores(
        query_embed, items_all, bias_all, codes_all, columns, positive_index, pos_codes
    )
    row_max, row_sum = partial_stats(scores)
    dlogit = finish(scores, row_max, row_sum, columns, positive_index, query_weights)
    query_grad = (
        score_scale * jnp.dot(dlogit, items_all, preferred_element_type=jnp.float32)
    ).astype(jnp.bfloat16)
    item_grad = lax.psum_scatter(
        score_scale
        * lax.dot_general(
            dlogit, query_embed, (((0,), (0,)), ((), ())), preferred_element_type=jnp.float32
        ),
        ("dp", "grp"),
        scatter_dimension=0,
        tiled=True,
    ).astype(jnp.bfloat16)
    query_in_part, query_out_part = tower_back(
        query_features, query_pre, query_hidden, query_w_out, query_grad
    )
    item_in_part, item_out_part = tower_back(
        item_features, item_pre, item_hidden, item_w_out, item_grad
    )
    query_in_sum, query_out_sum, item_in_sum, item_out_sum = lax.psum(
        (query_in_part, query_out_part, item_in_part, item_out_part), ("dp", "grp")
    )
    factor = loss_scale / weight_total
    return (
        query_in_sum * factor,
        query_out_sum * factor,
        item_in_sum * factor,
        item_out_sum * factor,
    )


def solution(mesh):
    in_specs = (
        P(("dp", "grp"), None),
        P(("dp", "grp")),
        P(("dp", "grp")),
        P(("dp", "grp"), None),
        P(("dp", "grp")),
        P(("dp", "grp")),
        P(),
        P(),
        P(),
        P(),
    )
    out_specs = (P(), P(), P(), P())
    return jax.shard_map(
        on_device, mesh=mesh, in_specs=in_specs, out_specs=out_specs, check_vma=False
    )
```

profile of v0, /device:TPU:0, one launch (start us, length us, event | category | flops | bytes accessed | tf_op | source)
XLA Modules:
  0.0 457.4 jit_solution(10545431475410207212)
XLA Ops:
  7.2 0.0 reduce-scatter.2.cloned.1.call-start
  7.2 1.6 fusion.16
  8.8 1.2 convolution_convert_fusion.1
  10.0 43.9 %all_gather.10 = bf16[512,256]{1,0:T(8,128)(2,1)S(1)} all-gather(bf16[16,256]{1,0:T(8,128)(2,1)S(1)} %convolution_convert_fusion.1), channel_id=1, replica_groups=mesh['dp'=16,'grp'=2] {'dp','grp'}, dimensions={0}, use_global_device_ids=true | all-gather | bytes 270336 | tf_op jit(solution)/shard_map/all_gather | solution.py:75
  54.0 0.8 dynamic-update-slice
  54.8 36.8 %all-reduce = s32[512]{0:T(512)S(1)} all-reduce(s32[512]{0:T(512)S(1)} %dynamic-update-slice), channel_id=1, replica_groups=mesh['dp'=16,'grp'=2] {'dp','grp'}, use_global_device_ids=true, to_apply=%add | all-reduce | flops 512 | bytes 4096
  91.6 0.8 dynamic-update-slice.1
  92.5 41.1 %all-reduce.1 = bf16[512]{0:T(512)(128)(2,1)S(1)} all-reduce(bf16[512]{0:T(512)(128)(2,1)S(1)} %dynamic-update-slice.1), channel_id=1, replica_groups=mesh['dp'=16,'grp'=2] {'dp','grp'}, use_global_device_ids=true, to_apply=%add.1 | all-reduce | flops 512 | bytes 2048
  133.6 4.8 %multiply_convert_fusion.1 = (bf16[1024,1024]{1,0:T(8,128)(2,1)S(1)}, f32[1024,1024]{1,0:T(8,128)}) fusion(bf16[1024,512]{1,0:T(8,128)(2,1)S(1)} %copy-done, bf16[512,1024]{1,0:T(8,128)(2,1)} %param.16), kind=kOutput, calls=%fused_computation.1 | convolution fusion | flops 1078984704 | bytes 8388608 | tf_op jit(solution)/shard_map/dot_general | solution.py:16
  138.4 0.7 convolution_convert_fusion
  139.1 0.6 copy-done.7
  139.7 0.3 select_reduce_fusion
  140.0 0.8 fusion.15
  140.8 0.3 fusion.1
  141.2 0.7 multiply_convert_fusion.2
  141.8 1.2 convolution_multiply_fusion.1
  143.1 0.0 reduce-scatter.2.cloned.1.call-update
  143.1 0.0 all-reduce.5.cloned.1.call-start
  143.2 0.5 fusion.2
  143.7 1.1 copy-done.8
  144.7 1.7 fusion.17
  146.5 6.1 %convolution_bitcast_fusion.1 = f32[512,1024]{0,1:T(8,128)} fusion(bf16[1024,512]{1,0:T(8,128)(2,1)S(1)} %copy-done, f32[1024,1024]{1,0:T(8,128)} %get-tuple-element.13, bf16[1024,256]{1,0:T(8,128)(2,1)S(1)} %fusion.2, bf16[1024,256]{1,0:T(8,128)(2,1)S(1)} %copy-done.6), kind=kOutput, calls=%fused_computation.13 | convolution fusion | flops 1620049920 | bytes 8388608 | tf_op jit(solution)/shard_map/dot_general | solution.py:26
  152.5 126.6 %reduce-scatter.2.cloned.1.call-done = f32[16,256]{1,0:T(8,128)} async-done(((f32[512,256]{1,0:T(8,128)}), f32[16,256]{1,0:T(8,128)}) %reduce-scatter.2.cloned.1.call-update) | async-done | bytes 16400 | tf_op jit(solution)/shard_map/reduce_scatter | solution.py:89
  279.2 2.7 convolution_bitcast_fusion
  281.9 1.3 fusion.9
  283.3 0.6 convert_reduce_fusion
  283.9 38.4 %psum.36 = f32[]{:T(128)} all-reduce(f32[]{:T(128)} %convert_reduce_fusion), channel_id=1, replica_groups=mesh['dp'=16,'grp'=2] {'dp','grp'}, use_global_device_ids=true, to_apply=%region_5.6 | all-reduce | flops 1 | bytes 8 | tf_op jit(solution)/shard_map/psum | solution.py:71
  322.9 115.9 %all-reduce.5.cloned.1.call-done = (f32[512,1024]{0,1:T(8,128)}, f32[1024,256]{1,0:T(8,128)}, f32[512,1024]{0,1:T(8,128)}, f32[1024,256]{1,0:T(8,128)}) async-done(((f32[512,1024]{0,1:T(8,128)}, f32[1024,256]{1,0:T(8,128)}, f32[512,1024]{0,1:T(8,128)}, f32[1024,256]{1,0:T(8,128)}), (f32[512,1024]{0,1:T(8,128)}, f32[1024,256]{1,0:T(8,128)}, f32[512,1024]{0,1:T(8,128)}, ...) | async-done | bytes 6291472 | tf_op jit(solution)/shard_map/psum | solution.py:104
  438.8 4.0 broadcast_multiply_fusion
  442.9 2.9 copy.14
  445.8 1.8 copy.15
  447.6 3.0 broadcast_multiply_fusion.2
  (22 shorter events, 0.1 us)
Async XLA Ops:
  7.2 126.5 %copy-start = (bf16[1024,512]{1,0:T(8,128)(2,1)S(1)}, bf16[1024,512]{1,0:T(8,128)(2,1)}, u32[]{:S(2)}) copy-start(bf16[1024,512]{1,0:T(8,128)(2,1)} %param.10) | copy-start | bytes 3145732
  7.2 272.0 %reduce-scatter.2.cloned.1.call-start = ((), (), s32[]{:S(2)}) async-start(), calls=%async_computation.1 | async-start | bytes 540672 | tf_op jit(solution)/shard_map/reduce_scatter | solution.py:89
  133.6 4.8 %copy-start.6 = (bf16[1024,256]{1,0:T(8,128)(2,1)S(1)}, bf16[1024,256]{1,0:T(8,128)(2,1)}, u32[]{:S(2)}) copy-start(bf16[1024,256]{1,0:T(8,128)(2,1)} %param.17) | copy-start | bytes 1572868
  138.4 1.3 copy-start.7
  138.4 1.3 copy-start.4
  140.0 0.8 copy-start.5
  143.1 295.7 %all-reduce.5.cloned.1.call-start = ((), (), s32[]{:S(2)}) async-start(), calls=%async_computation.2 | async-start | bytes 12582912 | tf_op jit(solution)/shard_map/psum | solution.py:104
  143.2 1.6 copy-start.8
  146.5 132.7 %copy-start.1 = (bf16[1024,256]{1,0:T(8,128)(2,1)S(1)}, bf16[1024,256]{1,0:T(8,128)(2,1)}, u32[]{:S(2)}) copy-start(bf16[1024,256]{1,0:T(8,128)(2,1)} %param.19) | copy-start | bytes 1572868
  146.5 132.7 %copy-start.2 = (bf16[16,512]{1,0:T(8,128)(2,1)S(1)}, bf16[16,512]{1,0:T(8,128)(2,1)}, u32[]{:S(2)}) copy-start(bf16[16,512]{1,0:T(8,128)(2,1)} %param.13) | copy-start | bytes 49156
  279.2 2.8 copy-start.3
Sparse Core Ops, SparseCore 0:
  143.2 135.9 reduce-scatter.1
  285.8 153.0 all-reduce.4
where the time goes:
time: 458 us; the launch traced here: 457 us
  waiting for transfers between devices  243 us (53%)
  blocking collectives  160 us (35%)
  matrix products  22.6 us (5%)
  between operations  14.8 us (3%)
  other arithmetic  8.95 us (2%)
  local copies, waits for them, and re-layouts  8.09 us (2%)
    reduce_scatter x1, waiting for transfers between devices, on_device(): lax.psum_scatter(score_scale * lax.dot_general(dlogit, query_embed, (((0,...  127 us
    psum x1, waiting for transfers between devices, on_device(): lax.psum((query_in_part, query_out_part, item_in_part, item_out_part), ('...  116 us
    unnamed x2, blocking collectives  78 us
    all_gather x1, blocking collectives, on_device(): lax.all_gather(item_embed, ('dp', 'grp'), axis=0, tiled=True)  43.9 us
    psum x1, blocking collectives, on_device(): weight_total = lax.psum(weight_part, ('dp', 'grp'))  38.4 us
  transfers between devices with their start and end apart: 2, of which 2 were waited for; matrix products, arithmetic and copies ran while one was open for 2% of the time, Pallas kernels for 0%

commit v1 on v0

v1 whole, which is shorter than its diff:
```python
import functools

import jax
import jax.numpy as jnp
from jax import lax
from jax.experimental import pallas as pl
from jax.experimental.pallas import tpu as pltpu
from jax.sharding import PartitionSpec as P

MESH = pl.DeviceIdType.MESH
F32 = jnp.float32
BF16 = jnp.bfloat16
SCALE = 0.25
LOSS = 1024.0
NN = (((1,), (0,)), ((), ()))
NT = (((1,), (1,)), ((), ()))
TN = (((0,), (0,)), ((), ()))


def dot(a, b, dims=NN):
    return lax.dot_general(a, b, dims, preferred_element_type=F32)


def gate_of(v):
    return 1.0 / (1.0 + jnp.exp(-v))


def kernel(
    D, k, QT, AT, CW, PR,
    qf, qw, pos, feat, ids, logq, wqi, wqo, wii, wio,
    oqi, oqo, oii, oio, ofac,
    feats, meta, slope, hid, hidT, qfT, qemb, qgrad, iemb, igrad, buf, rcv, gat,
    ag_send, ag_recv, mt_send, mt_recv, pair_send, pair_recv,
    rs_send, rs_recv, fg_send, fg_recv,
):
    dp = lax.axis_index("dp")
    grp = lax.axis_index("grp")
    Q, FE = qf.shape
    H, E = wqo.shape
    NI = feat.shape[0]
    I = D * 2 * NI
    other = 1 - grp
    n_item = I // PR
    n_out = H // PR
    n_in = H // CW
    parts = n_item + n_out + n_in

    barrier = pltpu.get_barrier_semaphore()

    def greet(o, c):
        pl.semaphore_signal(barrier, inc=1, device_id=(lax.rem(dp + o, D), grp), device_id_type=MESH)
        return c

    lax.fori_loop(1, D, greet, 0)
    pl.semaphore_signal(barrier, inc=1, device_id=(dp, other), device_id_type=MESH)

    feats[dp, grp] = feat[...]
    eye = lax.broadcasted_iota(jnp.int32, (NI, NI), 0) == lax.broadcasted_iota(jnp.int32, (NI, NI), 1)
    id_col = jnp.sum(jnp.where(eye, ids[...].astype(F32), 0.0), axis=1, keepdims=True)
    lq_col = jnp.sum(jnp.where(eye, logq[...].astype(F32), 0.0), axis=1, keepdims=True)
    w_sum = jnp.sum(qw[...].astype(F32), axis=1, keepdims=True)
    lane = lax.broadcasted_iota(jnp.int32, (NI, 128), 1)
    meta[dp, grp] = jnp.where(lane == 0, id_col, jnp.where(lane == 1, lq_col, jnp.where(lane == 2, w_sum, 0.0)))

    pl.semaphore_wait(barrier, D)

    def ag_copies(o):
        to = (lax.rem(dp + o, D), grp)
        a = pltpu.make_async_remote_copy(
            src_ref=feat, dst_ref=feats.at[dp, grp], send_sem=ag_send.at[o], recv_sem=ag_recv.at[o],
            device_id=to, device_id_type=MESH)
        b = pltpu.make_async_remote_copy(
            src_ref=meta.at[dp, grp], dst_ref=meta.at[dp, grp], send_sem=mt_send.at[o], recv_sem=mt_recv.at[o],
            device_id=to, device_id_type=MESH)
        return a, b

    def ag_start(o, c):
        a, b = ag_copies(o)
        a.start()
        b.start()
        return c

    lax.fori_loop(1, D, ag_start, 0)

    def forward(t, c):
        rows = pl.ds(pl.multiple_of(t * QT, QT), QT)
        pre = dot(qf[rows, :], wqi[...])
        g = gate_of(pre)
        h = (pre * g).astype(BF16)
        slope[rows, :] = g * (1.0 + pre * (1.0 - g))
        hid[rows, :] = h
        qemb[rows, :] = dot(h, wqo[...]).astype(BF16)
        return c

    lax.fori_loop(0, Q // QT, forward, 0)
    hidT[...] = hid[...].T
    qfT[...] = qf[...].T

    def ag_wait(o, c):
        a, b = ag_copies(o)
        a.wait()
        b.wait()
        return c

    lax.fori_loop(1, D, ag_wait, 0)

    pair = (dp, other)
    pf = pltpu.make_async_remote_copy(
        src_ref=feats.at[:, grp], dst_ref=feats.at[:, grp], send_sem=pair_send.at[0], recv_sem=pair_recv.at[0],
        device_id=pair, device_id_type=MESH)
    pm = pltpu.make_async_remote_copy(
        src_ref=meta.at[:, grp], dst_ref=meta.at[:, grp], send_sem=pair_send.at[1], recv_sem=pair_recv.at[1],
        device_id=pair, device_id_type=MESH)
    pf.start()
    pm.start()
    pf.wait()
    pm.wait()

    for r in range(n_item):
        blk = D // n_item
        x = feats[r * blk:(r + 1) * blk].reshape(PR, FE)
        pre = dot(x, wii[...])
        h = (pre * gate_of(pre)).astype(BF16)
        iemb[r * PR:(r + 1) * PR, :] = dot(h, wio[...]).astype(BF16)

    info = meta[...].reshape(I, 128)
    id_all = info[:, 0:1]
    lq_all = info[:, 1:2]
    total = jnp.sum(info[:, 2:3], axis=0, keepdims=True) * (1.0 / NI)
    factor = LOSS / total
    ofac[...] = jnp.broadcast_to(factor, ofac.shape)

    def attend(t, c):
        rows = pl.ds(pl.multiple_of(t * AT, AT), AT)
        e_t = qemb[rows, :]
        s = SCALE * dot(iemb[...], e_t, NT) - lq_all
        hit = lax.broadcasted_iota(jnp.int32, (I, AT), 0) == pos[:, rows]
        pid = jnp.sum(jnp.where(hit, id_all, 0.0), axis=0, keepdims=True)
        s = jnp.where(jnp.logical_and(id_all == pid, jnp.logical_not(hit)), -jnp.inf, s)
        m = jnp.maximum(jnp.max(s, axis=0, keepdims=True), -1e30)
        ex = jnp.exp(s - m)
        inv = 1.0 / jnp.sum(ex, axis=0, keepdims=True)
        w = qw[:, rows].astype(F32)
        d = (w * (ex * inv - jnp.where(hit, 1.0, 0.0))).astype(BF16)
        term = dot(d, e_t)
        igrad[...] = jnp.where(t == 0, term, igrad[...] + term)
        qgrad[rows, :] = (SCALE * dot(d, iemb[...], TN)).astype(BF16)
        return c

    igrad[...] = jnp.zeros_like(igrad)
    lax.fori_loop(0, Q // AT, attend, 0)

    halves = 0
    while halves < k + 1 and PR >> (halves + 1) >= 16:
        halves += 1
    bits = list(range(k))
    turned = bits[2:] + bits[:2]
    orders = [bits, [bits[1], bits[0]] + bits[2:], turned, bits, [bits[1], bits[0]] + bits[2:], turned[:-2] + [turned[-1], turned[-2]]]

    def peer(bit):
        if bit < 0:
            return grp, (dp, other)
        one = 1 << bit
        mine = lax.rem(lax.div(dp, one), 2)
        return mine, (dp + one * (1 - 2 * mine), grp)

    def plan(p):
        steps, off, rows = [], 0, PR
        slot = 0
        for s, bit in enumerate([-1] + orders[p % 6]):
            mine, to = peer(bit)
            if s < halves:
                rows //= 2
                send, off = off + (1 - mine) * rows, off + mine * rows
                steps.append((True, rows, send, off, slot, to))
            else:
                steps.append((False, rows, off, off, slot, to))
            slot += max(rows, 16)
        return steps

    plans = [plan(p) for p in range(parts)]

    def at(off, rows):
        return pl.ds(pl.multiple_of(off, 16), rows)

    def rs_copy(p, s):
        half, rows, send, keep, slot, to = plans[p][s]
        return pltpu.make_async_remote_copy(
            src_ref=buf.at[p, at(send, rows)],
            dst_ref=rcv.at[p, pl.ds(slot, rows)],
            send_sem=rs_send.at[p, s], recv_sem=rs_recv.at[p, s], device_id=to, device_id_type=MESH)

    def fg_copy(p, s):
        half, rows, send, keep, slot, to = plans[p][s]
        return pltpu.make_async_remote_copy(
            src_ref=gat.at[p, at(keep, rows)], dst_ref=gat.at[p, at(keep, rows)],
            send_sem=fg_send.at[p, s], recv_sem=fg_recv.at[p, s], device_id=to, device_id_type=MESH)

    last = k

    def advance(p, n):
        if n == 0:
            rs_copy(p, 0).start()
        elif n <= last + 1:
            s = n - 1
            rs_copy(p, s).wait()
            half, rows, send, keep, slot, to = plans[p][s]
            got = buf[p, at(keep, rows)].astype(F32) + rcv[p, pl.ds(slot, rows)].astype(F32)
            if s < last:
                buf[p, at(keep, rows)] = got.astype(BF16)
                rs_copy(p, s + 1).start()
            else:
                gat[p, at(keep, rows)] = got.astype(BF16)
                fg_copy(p, halves - 1).start()
        else:
            s = halves - 1 - (n - last - 2)
            fg_copy(p, s).wait()
            if s > 0:
                fg_copy(p, s - 1).start()

    turns = last + 2 + halves
    items = range(n_item)
    outs = range(n_item, n_item + n_out)
    ins = range(n_item + n_out, parts)

    for p in items:
        buf[p] = (SCALE * igrad[p * PR:(p + 1) * PR, :]).astype(BF16)
        advance(p, 0)
    step_i = 1

    g_out = dot(hidT[...], qgrad[...])
    for j, p in enumerate(outs):
        buf[p] = g_out[j * PR:(j + 1) * PR, :].astype(BF16)
        advance(p, 0)
    for p in items:
        advance(p, step_i)
    step_i += 1

    for j, p in enumerate(ins):
        cols = slice(j * CW, (j + 1) * CW)
        hg = dot(qgrad[...], wqo[cols, :], NT)
        pg = (hg * slope[:, cols]).astype(BF16)
        buf[p] = dot(qfT[...], pg).astype(BF16)
        advance(p, 0)
        for q in items:
            advance(q, step_i)
        step_i += 1

    def item_back(j):
        cols = slice(j * CW, (j + 1) * CW)
        x = feats[...].reshape(I, FE)
        ig = gat[0:n_item].reshape(I, E)
        pre = dot(x, wii[:, cols])
        g = gate_of(pre)
        h = (pre * g).astype(BF16)
        oio[cols, :] = dot(h, ig, TN)
        hg = dot(ig, wio[cols, :], NT)
        pg = (hg * (g * (1.0 + pre * (1.0 - g)))).astype(BF16)
        oii[:, cols] = dot(x, pg, TN)

    done = 0
    for n in range(1, turns):
        for p in list(outs) + list(ins):
            advance(p, n)
        for _ in range(2):
            if step_i < turns:
                for q in items:
                    advance(q, step_i)
                step_i += 1
        if step_i >= turns and done < n_in:
            item_back(done)
            done += 1
    while done < n_in:
        item_back(done)
        done += 1

    for j, p in enumerate(outs):
        oqo[j * PR:(j + 1) * PR, :] = gat[p]
    for j, p in enumerate(ins):
        oqi[:, j * CW:(j + 1) * CW] = gat[p]


def solution(mesh):
    D = mesh.shape["dp"]
    k = D.bit_length() - 1

    def on_device(qf, qw, pos, feat, ids, logq, wqi, wqo, wii, wio):
        Q, FE = qf.shape
        H, E = wqo.shape
        NI = feat.shape[0]
        I = NI * D * 2
        QT, CW, PR = 256, E, FE
        AT = QT if I <= 4 * QT else QT // 2
        parts = I // PR + H // PR + H // CW
        vm = pl.BlockSpec(memory_space=pltpu.VMEM)
        dma = pltpu.SemaphoreType.DMA
        oqi, oqo, oii, oio, fac = pl.pallas_call(
            functools.partial(kernel, D, k, QT, AT, CW, PR),
            name="retrieval_grads",
            out_shape=(
                jax.ShapeDtypeStruct((FE, H), BF16),
                jax.ShapeDtypeStruct((H, E), BF16),
                jax.ShapeDtypeStruct((FE, H), F32),
                jax.ShapeDtypeStruct((H, E), F32),
                jax.ShapeDtypeStruct((8, 128), F32),
            ),
            in_specs=[vm] * 10,
            out_specs=(vm,) * 5,
            scratch_shapes=[
                pltpu.VMEM((D, 2, NI, FE), BF16),
                pltpu.VMEM((D, 2, NI, 128), F32),
                pltpu.VMEM((Q, H), F32),
                pltpu.VMEM((Q, H), BF16),
                pltpu.VMEM((H, Q), BF16),
                pltpu.VMEM((FE, Q), BF16),
                pltpu.VMEM((Q, E), BF16),
                pltpu.VMEM((Q, E), BF16),
                pltpu.VMEM((I, E), BF16),
                pltpu.VMEM((I, E), F32),
                pltpu.VMEM((parts, PR, E), BF16),
                pltpu.VMEM((parts, PR + 64, E), BF16),
                pltpu.VMEM((parts, PR, E), BF16),
                dma((D,)), dma((D,)), dma((D,)), dma((D,)), dma((2,)), dma((2,)),
                dma((parts, k + 1)), dma((parts, k + 1)), dma((parts, k + 1)), dma((parts, k + 1)),
            ],
            compiler_params=pltpu.CompilerParams(
                collective_id=0, has_side_effects=True, vmem_limit_bytes=(48 if I <= 4 * QT else 62) * 1024 * 1024),
        )(qf, qw.reshape(1, Q), pos.reshape(1, Q), feat, ids.reshape(1, NI), logq.reshape(1, NI), wqi, wqo, wii, wio)
        f = fac[0, 0]
        return (oqi.astype(F32) * f, oqo.astype(F32) * f, oii * f, oio * f)

    rows = P(("dp", "grp"), None)
    flat = P(("dp", "grp"))
    return jax.shard_map(
        on_device, mesh=mesh,
        in_specs=(rows, flat, flat, rows, flat, flat, P(), P(), P(), P()),
        out_specs=(P(), P(), P(), P()),
        check_vma=False,
    )
```

time: 458 us -> 90.8 us (0.20)
  waiting for transfers between devices: 243 us -> 0 us
  blocking collectives: 160 us -> 0 us
  Pallas kernels: 0 us -> 74 us
  matrix products: 22.6 us -> 0 us
  between operations: 14.8 us -> 0.65 us
    reduce_scatter x1 -> x0, waiting for transfers between devices: 127 us -> none  [on_device(): lax.psum_scatter(score_scale * lax.dot_general(dlogit, query_embed, (((0,...]
    psum x1 -> x0, waiting for transfers between devices: 116 us -> none  [on_device(): lax.psum((query_in_part, query_out_part, item_in_part, item_out_part), ('...]
    unnamed x2 -> x0, blocking collectives: 78 us -> none
    pallas_call x0 -> x1, Pallas kernels: none -> 74 us  [on_device(): pl.pallas_call(functools.partial(kernel, D, k, QT, AT, CW, PR), name='ret...]
    all_gather x1 -> x0, blocking collectives: 43.9 us -> none  [on_device(): lax.all_gather(item_embed, ('dp', 'grp'), axis=0, tiled=True)]
    psum x1 -> x0, blocking collectives: 38.4 us -> none  [on_device(): weight_total = lax.psum(weight_part, ('dp', 'grp'))]
    dot_general x11 -> x0, matrix products: 22.6 us -> none  [the longest x2 8.81 us: tower_back(): grad_in = jnp.dot(features.T, pre_grad, preferred_element_type=jnp.float32)]
  transfers between devices with their start and end apart: 2 -> 0, of which waited for: 2 -> 0; matrix products, arithmetic and copies ran while one was open for 2% -> 0% of each run, Pallas kernels for 0% -> 0%
where the time goes in v1:
time: 90.8 us; the launch traced here: 90.3 us
  Pallas kernels  74 us (81%)
  local copies, waits for them, and re-layouts  8.51 us (9%)
  other arithmetic  7.16 us (8%)
    pallas_call x1, Pallas kernels, on_device(): pl.pallas_call(functools.partial(kernel, D, k, QT, AT, CW, PR), name='ret...  74 us
    unnamed x16, local copies, waits for them, and re-layouts  7.24 us
    mul x2, other arithmetic, on_device(): return (oqi.astype(F32) * f, oqo.astype(F32) * f, oii * f, oio * f)  7.16 us

profile of v1, /device:TPU:0, one launch (start us, length us, event | category | flops | bytes accessed | tf_op | source)
XLA Modules:
  0.0 90.3 jit_solution(13360438197477364676)
XLA Ops:
  0.6 0.7 reshape.20.qw
  1.3 0.0 copy-start
  1.3 1.2 %copy-done = bf16[1024,512]{1,0:T(8,128)(2,1)S(1)} copy-done((bf16[1024,512]{1,0:T(8,128)(2,1)S(1)}, bf16[1024,512]{1,0:T(8,128)(2,1)}, u32[]{:S(2)}) %copy-start) | copy-done | bytes 1048600
  2.5 0.0 copy-start.1
  2.5 1.2 %copy-done.1 = bf16[512,1024]{1,0:T(8,128)(2,1)S(1)} copy-done((bf16[512,1024]{1,0:T(8,128)(2,1)S(1)}, bf16[512,1024]{1,0:T(8,128)(2,1)}, u32[]{:S(2)}) %copy-start.1) | copy-done | bytes 1048600
  3.8 0.0 copy-start.2
  3.8 1.0 %copy-done.2 = bf16[1024,256]{1,0:T(8,128)(2,1)S(1)} copy-done((bf16[1024,256]{1,0:T(8,128)(2,1)S(1)}, bf16[1024,256]{1,0:T(8,128)(2,1)}, u32[]{:S(2)}) %copy-start.2) | copy-done | bytes 524312
  4.8 0.0 copy-start.3
  4.8 1.0 %copy-done.3 = bf16[1024,256]{1,0:T(8,128)(2,1)S(1)} copy-done((bf16[1024,256]{1,0:T(8,128)(2,1)S(1)}, bf16[1024,256]{1,0:T(8,128)(2,1)}, u32[]{:S(2)}) %copy-start.3) | copy-done | bytes 524312
  5.9 0.0 copy-start.4
  5.9 0.7 copy-done.4
  6.6 0.0 copy-start.5
  6.6 0.7 copy-done.5
  7.3 0.0 copy-start.6
  7.3 0.7 copy-done.6
  7.9 0.0 copy-start.7
  7.9 0.7 copy-done.7
  8.6 74.0 %retrieval_grads.1 = (bf16[512,1024]{1,0:T(8,128)(2,1)S(1)}, bf16[1024,256]{1,0:T(8,128)(2,1)S(1)}, f32[512,1024]{1,0:T(8,128)}, f32[1024,256]{1,0:T(8,128)S(1)}, f32[8,128]{1,0:T(8,128)S(1)}) custom-call(bf16[1024,512]{1,0:T(8,128)(2,1)S(1)} %copy-done, bf16[1,1024]{1,0:T(2,128)(2,1)S(1)} %reshape.20.qw, s32[1,1024]{1,0:T(1,128)S(1)} %bitcast.4, ...), custom_call_target="tpu_custom_call" | custom-call | tf_op jit(solution)/shard_map/retrieval_grads/pallas_call | solution.py:297
  82.5 0.6 slice.3
  83.1 5.0 %convert_multiply_fusion = (f32[512,1024]{1,0:T(8,128)}, f32[512,1024]{1,0:T(8,128)}) fusion(bf16[512,1024]{1,0:T(8,128)(2,1)S(1)} %get-tuple-element.9, f32[]{:T(128)} %bitcast.3, f32[512,1024]{1,0:T(8,128)} %get-tuple-element.12), kind=kLoop, calls=%fused_computation | loop fusion | flops 1572864 | bytes 7340036 | tf_op jit(solution)/shard_map/mul | solution.py:330
  88.1 2.2 %convert_multiply_fusion.1 = (f32[1024,256]{1,0:T(8,128)}, f32[1024,256]{1,0:T(8,128)}) fusion(bf16[1024,256]{1,0:T(8,128)(2,1)S(1)} %get-tuple-element.11, f32[]{:T(128)} %bitcast.3, f32[1024,256]{1,0:T(8,128)S(1)} %get-tuple-element.13), kind=kLoop, calls=%fused_computation.1 | loop fusion | flops 786432 | bytes 3670020 | tf_op jit(solution)/shard_map/mul | solution.py:330
Async XLA Ops:
  1.3 1.2 %copy-start = (bf16[1024,512]{1,0:T(8,128)(2,1)S(1)}, bf16[1024,512]{1,0:T(8,128)(2,1)}, u32[]{:S(2)}) copy-start(bf16[1024,512]{1,0:T(8,128)(2,1)} %qf.1) | copy-start | bytes 3145732
  2.5 1.2 %copy-start.1 = (bf16[512,1024]{1,0:T(8,128)(2,1)S(1)}, bf16[512,1024]{1,0:T(8,128)(2,1)}, u32[]{:S(2)}) copy-start(bf16[512,1024]{1,0:T(8,128)(2,1)} %wqi.1) | copy-start | bytes 3145732
  3.8 1.0 %copy-start.2 = (bf16[1024,256]{1,0:T(8,128)(2,1)S(1)}, bf16[1024,256]{1,0:T(8,128)(2,1)}, u32[]{:S(2)}) copy-start(bf16[1024,256]{1,0:T(8,128)(2,1)} %wqo.1) | copy-start | bytes 1572868
  4.8 1.0 %copy-start.3 = (bf16[1024,256]{1,0:T(8,128)(2,1)S(1)}, bf16[1024,256]{1,0:T(8,128)(2,1)}, u32[]{:S(2)}) copy-start(bf16[1024,256]{1,0:T(8,128)(2,1)} %wio.1) | copy-start | bytes 1572868
  5.9 0.7 copy-start.4
  6.6 0.7 copy-start.5
  7.3 0.7 copy-start.6
  7.9 0.7 copy-start.7

commit v2 on v1

v2 whole, which is shorter than its diff:
```python
import functools

import jax
import jax.numpy as jnp
from jax import lax
from jax.experimental import pallas as pl
from jax.experimental.pallas import tpu as pltpu
from jax.sharding import PartitionSpec as P

MESH = pl.DeviceIdType.MESH
F32 = jnp.float32
BF16 = jnp.bfloat16
SCALE = 0.25
LOSS = 1024.0
NN = (((1,), (0,)), ((), ()))
NT = (((1,), (1,)), ((), ()))
TN = (((0,), (0,)), ((), ()))


def dot(a, b, dims=NN):
    return lax.dot_general(a, b, dims, preferred_element_type=F32)


def gate_of(v):
    return 1.0 / (1.0 + jnp.exp(-v))


def kernel(
    D, k, QT, AT, CW, PR,
    qf_h, qw_h, pos_h, feat_h, ids_h, logq_h, wqi_h, wqo_h, wii_h, wio_h,
    oqi, oqo, oii, oio, ofac,
    qf, qw, pos, ids, logq, wqi, wqo, wii, wio, load,
    feats, meta, embs, slope, hid, hidT, qfT, qemb, qgrad, igrad, buf, rcv, gat,
    em_send, em_recv, ag_send, ag_recv, mt_send, mt_recv, pair_send, pair_recv,
    rs_send, rs_recv, fg_send, fg_recv,
):
    dp = lax.axis_index("dp")
    grp = lax.axis_index("grp")
    Q, FE = qf.shape
    H, E = wqo.shape
    NI = feat_h.shape[0]
    I = D * 2 * NI
    other = 1 - grp
    n_item = I // PR
    n_out = H // PR
    n_in = H // CW
    parts = n_item + n_out + n_in

    mine_at = feats.at[dp, grp]
    pairs = [(feat_h, mine_at), (wii_h, wii), (wio_h, wio), (ids_h, ids), (logq_h, logq), (qw_h, qw), (wqi_h, wqi),
             (qf_h, qf), (wqo_h, wqo), (pos_h, pos)]
    loads = [pltpu.make_async_copy(a, b, load.at[i]) for i, (a, b) in enumerate(pairs)]
    for c in loads:
        c.start()

    barrier = pltpu.get_barrier_semaphore()

    def greet(o, c):
        pl.semaphore_signal(barrier, inc=1, device_id=(lax.rem(dp + o, D), grp), device_id_type=MESH)
        return c

    lax.fori_loop(1, D, greet, 0)
    pl.semaphore_signal(barrier, inc=1, device_id=(dp, other), device_id_type=MESH)

    for c in loads[:6]:
        c.wait()
    i_pre = dot(mine_at[...], wii[...])
    embs[dp, grp] = dot((i_pre * gate_of(i_pre)).astype(BF16), wio[...]).astype(BF16)
    meta[dp, grp] = jnp.zeros((8, 128), F32)
    meta[dp, grp, 0:1, 0:NI] = ids[...].astype(F32)
    meta[dp, grp, 1:2, 0:NI] = logq[...].astype(F32)
    meta[dp, grp, 2:3, :] = jnp.broadcast_to(jnp.sum(qw[...].astype(F32), axis=1, keepdims=True), (1, 128))

    pl.semaphore_wait(barrier, D)

    def to_all(ref, send, recv):
        def copy(o):
            return pltpu.make_async_remote_copy(
                src_ref=ref.at[dp, grp], dst_ref=ref.at[dp, grp], send_sem=send.at[o], recv_sem=recv.at[o],
                device_id=(lax.rem(dp + o, D), grp), device_id_type=MESH)

        def start(o, c):
            copy(o).start()
            return c

        def wait(o, c):
            copy(o).wait()
            return c

        return (lambda: lax.fori_loop(1, D, start, 0)), (lambda: lax.fori_loop(1, D, wait, 0))

    def to_pair(ref, i):
        return pltpu.make_async_remote_copy(
            src_ref=ref.at[:, grp], dst_ref=ref.at[:, grp], send_sem=pair_send.at[i], recv_sem=pair_recv.at[i],
            device_id=(dp, other), device_id_type=MESH)

    emb_start, emb_wait = to_all(embs, em_send, em_recv)
    meta_start, meta_wait = to_all(meta, mt_send, mt_recv)
    feat_start, feat_wait = to_all(feats, ag_send, ag_recv)
    meta_start()
    emb_start()
    feat_start()

    for c in loads[6:9]:
        c.wait()

    def forward(t, c):
        rows = pl.ds(pl.multiple_of(t * QT, QT), QT)
        pre = dot(qf[rows, :], wqi[...])
        g = gate_of(pre)
        h = (pre * g).astype(BF16)
        slope[rows, :] = g * (1.0 + pre * (1.0 - g))
        hid[rows, :] = h
        qemb[rows, :] = dot(h, wqo[...]).astype(BF16)
        return c

    lax.fori_loop(0, Q // QT, forward, 0)
    hidT[...] = hid[...].T
    qfT[...] = qf[...].T

    loads[9].wait()
    meta_wait()
    pm = to_pair(meta, 0)
    pm.start()
    emb_wait()
    pe = to_pair(embs, 1)
    pe.start()
    pm.wait()
    pe.wait()

    diag = lax.broadcasted_iota(jnp.int32, (1, NI, 128), 1) == lax.broadcasted_iota(jnp.int32, (1, NI, 128), 2)

    def column(r):
        row = meta[:, :, r:r + 1, :].reshape(2 * D, 1, 128)
        return jnp.sum(jnp.where(diag, row, 0.0), axis=2, keepdims=True).reshape(I, 1)

    id_all = column(0)
    lq_all = column(1)
    total = jnp.sum(meta[:, :, 2:3, :].reshape(2 * D, 128)[:, 0:1], axis=0, keepdims=True)
    factor = LOSS / total
    ofac[...] = jnp.broadcast_to(factor, ofac.shape)

    def attend(t, c):
        rows = pl.ds(pl.multiple_of(t * AT, AT), AT)
        e_t = qemb[rows, :]
        i_emb = embs[...].reshape(I, E)
        s = SCALE * dot(i_emb, e_t, NT) - lq_all
        hit = lax.broadcasted_iota(jnp.int32, (I, AT), 0) == pos[:, rows]
        pid = jnp.sum(jnp.where(hit, id_all, 0.0), axis=0, keepdims=True)
        s = jnp.where(jnp.logical_and(id_all == pid, jnp.logical_not(hit)), -jnp.inf, s)
        m = jnp.maximum(jnp.max(s, axis=0, keepdims=True), -1e30)
        ex = jnp.exp(s - m)
        inv = 1.0 / jnp.sum(ex, axis=0, keepdims=True)
        w = qw[:, rows].astype(F32)
        d = (w * (ex * inv - jnp.where(hit, 1.0, 0.0))).astype(BF16)
        term = dot(d, e_t)
        igrad[...] = jnp.where(t == 0, term, igrad[...] + term)
        qgrad[rows, :] = (SCALE * dot(d, i_emb, TN)).astype(BF16)
        return c

    igrad[...] = jnp.zeros_like(igrad)
    lax.fori_loop(0, Q // AT, attend, 0)

    bits = list(range(k))
    tail = [[2, 3]] + [[b] for b in bits[4:]] if k >= 4 else [[b] for b in bits[2:]]
    heads = [[[b] for b in bits[:2]], [[b] for b in bits[:2][::-1]]]

    def plan(p):
        steps, off, rows, slot, sem = [], 0, PR, 0, 0
        for group in [None] + heads[p % 2] + tail:
            ways = 2 if group is None else 1 << len(group)
            one = 1 if group is None else 1 << group[0]
            digit = grp if group is None else lax.rem(lax.div(dp, one), ways)
            split = rows // ways >= 16
            size = rows // ways if split else rows
            moves = []
            for o in range(1, ways):
                there = lax.rem(digit + o, ways)
                to = (dp, there) if group is None else (dp + one * (there - digit), grp)
                moves.append((to, off + there * size if split else off, slot, sem))
                slot += size
                sem += 1
            off = off + digit * size if split else off
            rows = size
            steps.append((split, size, off, moves))
        return steps

    plans = [plan(p) for p in range(parts)]
    stages = len(plans[0])
    back = [s for s in range(stages) if plans[0][s][0]][::-1]
    turns = 1 + stages + len(back)

    def at(off, rows):
        return pl.ds(pl.multiple_of(off, 16), rows)

    def out_copies(p, s):
        split, size, keep, moves = plans[p][s]
        return [pltpu.make_async_remote_copy(
            src_ref=buf.at[p, at(send, size)], dst_ref=rcv.at[p, pl.ds(slot, size)],
            send_sem=rs_send.at[p, i], recv_sem=rs_recv.at[p, i], device_id=to, device_id_type=MESH)
            for to, send, slot, i in moves]

    def back_copies(p, s):
        split, size, keep, moves = plans[p][s]
        return [pltpu.make_async_remote_copy(
            src_ref=gat.at[p, at(keep, size)], dst_ref=gat.at[p, at(keep, size)],
            send_sem=fg_send.at[p, i], recv_sem=fg_recv.at[p, i], device_id=to, device_id_type=MESH)
            for to, send, slot, i in moves]

    def start(copies):
        for c in copies:
            c.start()

    def wait(copies):
        for c in copies:
            c.wait()

    def advance(p, n):
        if n == 0:
            start(out_copies(p, 0))
        elif n <= stages:
            s = n - 1
            wait(out_copies(p, s))
            split, size, keep, moves = plans[p][s]
            got = buf[p, at(keep, size)].astype(F32)
            for to, send, slot, i in moves:
                got = got + rcv[p, pl.ds(slot, size)].astype(F32)
            if n < stages:
                buf[p, at(keep, size)] = got.astype(BF16)
                start(out_copies(p, n))
            else:
                gat[p, at(keep, size)] = got.astype(BF16)
                start(back_copies(p, back[0]))
        else:
            i = n - stages - 1
            wait(back_copies(p, back[i]))
            if i + 1 < len(back):
                start(back_copies(p, back[i + 1]))
            elif p in outs:
                oqo[(p - outs[0]) * PR:(p - outs[0] + 1) * PR, :] = gat[p]
            elif p in ins:
                oqi[:, (p - ins[0]) * CW:(p - ins[0] + 1) * CW] = gat[p]

    items = range(n_item)
    outs = range(n_item, n_item + n_out)
    ins = range(n_item + n_out, parts)

    for p in items:
        buf[p] = (SCALE * igrad[p * PR:(p + 1) * PR, :]).astype(BF16)
        advance(p, 0)

    g_out = dot(hidT[...], qgrad[...])
    for j, p in enumerate(outs):
        buf[p] = g_out[j * PR:(j + 1) * PR, :].astype(BF16)
        advance(p, 0)
    for p in items:
        advance(p, 1)

    for j, p in enumerate(ins):
        cols = slice(j * CW, (j + 1) * CW)
        hg = dot(qgrad[...], wqo[cols, :], NT)
        pg = (hg * slope[:, cols]).astype(BF16)
        buf[p] = dot(qfT[...], pg).astype(BF16)
        advance(p, 0)
        if j == 1:
            for q in items:
                advance(q, 2)

    feat_wait()
    pf = to_pair(feats, 2)
    pf.start()
    step_i = 3

    def item_back(j):
        cols = slice(j * CW, (j + 1) * CW)
        x = feats[...].reshape(I, FE)
        ig = gat[0:n_item].reshape(I, E)
        pre = dot(x, wii[:, cols])
        g = gate_of(pre)
        h = (pre * g).astype(BF16)
        oio[cols, :] = dot(h, ig, TN) * factor
        hg = dot(ig, wio[cols, :], NT)
        pg = (hg * (g * (1.0 + pre * (1.0 - g)))).astype(BF16)
        oii[:, cols] = dot(x, pg, TN) * factor

    done = 0
    for n in range(1, turns):
        for p in list(outs) + list(ins):
            advance(p, n)
        if step_i < turns:
            for q in items:
                advance(q, step_i)
            step_i += 1
            if step_i == turns:
                pf.wait()
        elif done < n_in:
            for _ in range(2):
                item_back(done)
                done += 1
    while done < n_in:
        item_back(done)
        done += 1


def finish(qi, qo, ii, io, fac, gqi, gqo, gii, gio, bi, bo, sem):
    direct = [pltpu.make_async_copy(ii, gii, sem.at[0]), pltpu.make_async_copy(io, gio, sem.at[1])]
    for c in direct:
        c.start()
    f = fac[0:1, 0:1]
    bo[...] = qo[...].astype(F32) * f
    a = pltpu.make_async_copy(bo, gqo, sem.at[2])
    a.start()
    bi[...] = qi[...].astype(F32) * f
    b = pltpu.make_async_copy(bi, gqi, sem.at[3])
    b.start()
    for c in direct + [a, b]:
        c.wait()


def solution(mesh):
    D = mesh.shape["dp"]
    k = D.bit_length() - 1

    def on_device(qf, qw, pos, feat, ids, logq, wqi, wqo, wii, wio):
        Q, FE = qf.shape
        H, E = wqo.shape
        NI = feat.shape[0]
        I = NI * D * 2
        QT, CW, PR = 256, E, FE
        AT = QT if I <= 4 * QT else QT // 2
        parts = I // PR + H // PR + H // CW
        vm = pl.BlockSpec(memory_space=pltpu.VMEM)
        dma = pltpu.SemaphoreType.DMA
        args = (qf, qw.reshape(1, Q), pos.reshape(1, Q), feat, ids.reshape(1, NI), logq.reshape(1, NI), wqi, wqo, wii, wio)
        oqi, oqo, oii, oio, fac = pl.pallas_call(
            functools.partial(kernel, D, k, QT, AT, CW, PR),
            name="retrieval_grads",
            out_shape=(
                jax.ShapeDtypeStruct((FE, H), BF16),
                jax.ShapeDtypeStruct((H, E), BF16),
                jax.ShapeDtypeStruct((FE, H), F32),
                jax.ShapeDtypeStruct((H, E), F32),
                jax.ShapeDtypeStruct((8, 128), F32),
            ),
            in_specs=[pl.BlockSpec(memory_space=pltpu.HBM)] * 10,
            out_specs=(vm,) * 5,
            scratch_shapes=[
                pltpu.VMEM((Q, FE), BF16), pltpu.VMEM((1, Q), BF16), pltpu.VMEM((1, Q), jnp.int32),
                pltpu.VMEM((1, NI), jnp.int32), pltpu.VMEM((1, NI), BF16),
                pltpu.VMEM((FE, H), BF16), pltpu.VMEM((H, E), BF16), pltpu.VMEM((FE, H), BF16), pltpu.VMEM((H, E), BF16),
                dma((10,)),
                pltpu.VMEM((D, 2, NI, FE), BF16),
                pltpu.VMEM((D, 2, 8, 128), F32),
                pltpu.VMEM((D, 2, NI, E), BF16),
                pltpu.VMEM((Q, H), F32),
                pltpu.VMEM((Q, H), BF16),
                pltpu.VMEM((H, Q), BF16),
                pltpu.VMEM((FE, Q), BF16),
                pltpu.VMEM((Q, E), BF16),
                pltpu.VMEM((Q, E), BF16),
                pltpu.VMEM((I, E), F32),
                pltpu.VMEM((parts, PR, E), BF16),
                pltpu.VMEM((parts, PR + 64, E), BF16),
                pltpu.VMEM((parts, PR, E), BF16),
                dma((D,)), dma((D,)), dma((D,)), dma((D,)), dma((D,)), dma((D,)), dma((3,)), dma((3,)),
                dma((parts, 2 * k + 2)), dma((parts, 2 * k + 2)), dma((parts, 2 * k + 2)), dma((parts, 2 * k + 2)),
            ],
            compiler_params=pltpu.CompilerParams(
                collective_id=0, has_side_effects=True, vmem_limit_bytes=(48 if I <= 4 * QT else 62) * 1024 * 1024),
        )(*[pltpu.with_memory_space_constraint(v, pltpu.HBM) for v in args])
        hbm = pl.BlockSpec(memory_space=pltpu.HBM)
        return tuple(pl.pallas_call(
            finish,
            name="finish",
            out_shape=(
                jax.ShapeDtypeStruct((FE, H), F32),
                jax.ShapeDtypeStruct((H, E), F32),
                jax.ShapeDtypeStruct((FE, H), F32),
                jax.ShapeDtypeStruct((H, E), F32),
            ),
            in_specs=[vm] * 5,
            out_specs=(hbm,) * 4,
            scratch_shapes=[pltpu.VMEM((FE, H), F32), pltpu.VMEM((H, E), F32), pltpu.SemaphoreType.DMA((4,))],
            compiler_params=pltpu.CompilerParams(vmem_limit_bytes=8 * 1024 * 1024),
        )(oqi, oqo, oii, oio, fac))

    rows = P(("dp", "grp"), None)
    flat = P(("dp", "grp"))
    return jax.shard_map(
        on_device, mesh=mesh,
        in_specs=(rows, flat, flat, rows, flat, flat, P(), P(), P(), P()),
        out_specs=(P(), P(), P(), P()),
        check_vma=False,
    )
```

time: 90.8 us -> 63.4 us (0.70)
  Pallas kernels: 74 us -> 61.2 us
  local copies, waits for them, and re-layouts: 8.51 us -> 1.28 us
  other arithmetic: 7.16 us -> 0 us
    pallas_call x1, Pallas kernels: 74 us -> 58.5 us  [on_device(): pl.pallas_call(functools.partial(kernel, D, k, QT, AT, CW, PR), name='ret...]
    unnamed x16 -> x0, local copies, waits for them, and re-layouts: 7.24 us -> none
    mul x2 -> x0, other arithmetic: 7.16 us -> none  [on_device(): return (oqi.astype(F32) * f, oqo.astype(F32) * f, oii * f, oio * f)]
    pallas_call x0 -> x1, Pallas kernels: none -> 2.74 us  [on_device(): pl.pallas_call(finish, name='finish', out_shape=(jax.ShapeDtypeStruct((FE...]
where the time goes in v2:
time: 63.4 us; the launch traced here: 63.1 us
  Pallas kernels  61.2 us (97%)
  local copies, waits for them, and re-layouts  1.28 us (2%)
  between operations  0.64 us (1%)
    pallas_call x1, Pallas kernels, on_device(): pl.pallas_call(functools.partial(kernel, D, k, QT, AT, CW, PR), name='ret...  58.5 us
    pallas_call x1, Pallas kernels, on_device(): pl.pallas_call(finish, name='finish', out_shape=(jax.ShapeDtypeStruct((FE...  2.74 us
    reshape x1, local copies, waits for them, and re-layouts, on_device(): qw.reshape(1, Q)  1.28 us

profile of v2, /device:TPU:0, one launch (start us, length us, event | category | flops | bytes accessed | tf_op | source)
XLA Modules:
  0.0 63.1 jit_solution(5500252599420936816)
XLA Ops:
  0.6 1.3 %reshape.20.qw_h = bf16[1,1024]{1,0:T(2,128)(2,1)} reshape(bf16[1024]{0:T(1024)(128)(2,1)} %param.11) | data formatting | bytes 4096 | tf_op jit(solution)/shard_map/reshape | solution.py:334
  1.9 58.5 %retrieval_grads.1 = (bf16[512,1024]{1,0:T(8,128)(2,1)S(1)}, bf16[1024,256]{1,0:T(8,128)(2,1)S(1)}, f32[512,1024]{1,0:T(8,128)S(1)}, f32[1024,256]{1,0:T(8,128)S(1)}, f32[8,128]{1,0:T(8,128)S(1)}) custom-call(bf16[1024,512]{1,0:T(8,128)(2,1)} %qf_h.1, bf16[1,1024]{1,0:T(2,128)(2,1)} %reshape.20.qw_h, s32[1,1024]{1,0:T(1,128)} %bitcast.3, ...), custom_call_target="tpu_custom_call" | custom-call | tf_op jit(solution)/shard_map/retrieval_grads/pallas_call | solution.py:335
  60.4 2.7 %finish.1 = (f32[512,1024]{1,0:T(8,128)}, f32[1024,256]{1,0:T(8,128)}, f32[512,1024]{1,0:T(8,128)}, f32[1024,256]{1,0:T(8,128)}) custom-call(bf16[512,1024]{1,0:T(8,128)(2,1)S(1)} %get-tuple-element.9.qi, bf16[1024,256]{1,0:T(8,128)(2,1)S(1)} %get-tuple-element.10.qo, f32[512,1024]{1,0:T(8,128)S(1)} %get-tuple-element.11.ii, ...), custom_call_target="tpu_custom_call" | custom-call | tf_op jit(solution)/shard_map/finish/pallas_call | solution.py:372

commit v3 on v2

--- a/solution.py
+++ b/solution.py
@@ -30,7 +30,7 @@
     qf_h, qw_h, pos_h, feat_h, ids_h, logq_h, wqi_h, wqo_h, wii_h, wio_h,
     oqi, oqo, oii, oio, ofac,
     qf, qw, pos, ids, logq, wqi, wqo, wii, wio, load,
-    feats, meta, embs, slope, hid, hidT, qfT, qemb, qgrad, igrad, buf, rcv, gat,
+    feats, meta, embs, slope, hid, hidT, qfT, qemb, qgrad, wrow, igrad, buf, rcv, gat,
     em_send, em_recv, ag_send, ag_recv, mt_send, mt_recv, pair_send, pair_recv,
     rs_send, rs_recv, fg_send, fg_recv,
 ):
@@ -64,12 +64,13 @@
 
     for c in loads[:6]:
         c.wait()
+    wrow[...] = qw[...].astype(F32).reshape(1, Q)
     i_pre = dot(mine_at[...], wii[...])
     embs[dp, grp] = dot((i_pre * gate_of(i_pre)).astype(BF16), wio[...]).astype(BF16)
     meta[dp, grp] = jnp.zeros((8, 128), F32)
     meta[dp, grp, 0:1, 0:NI] = ids[...].astype(F32)
     meta[dp, grp, 1:2, 0:NI] = logq[...].astype(F32)
-    meta[dp, grp, 2:3, :] = jnp.broadcast_to(jnp.sum(qw[...].astype(F32), axis=1, keepdims=True), (1, 128))
+    meta[dp, grp, 2:3, :] = jnp.broadcast_to(jnp.sum(wrow[...], axis=1, keepdims=True), (1, 128))
 
     pl.semaphore_wait(barrier, D)
 
@@ -151,7 +152,7 @@
         m = jnp.maximum(jnp.max(s, axis=0, keepdims=True), -1e30)
         ex = jnp.exp(s - m)
         inv = 1.0 / jnp.sum(ex, axis=0, keepdims=True)
-        w = qw[:, rows].astype(F32)
+        w = wrow[:, rows]
         d = (w * (ex * inv - jnp.where(hit, 1.0, 0.0))).astype(BF16)
         term = dot(d, e_t)
         igrad[...] = jnp.where(t == 0, term, igrad[...] + term)
@@ -162,12 +163,18 @@
     lax.fori_loop(0, Q // AT, attend, 0)
 
     bits = list(range(k))
-    tail = [[2, 3]] + [[b] for b in bits[4:]] if k >= 4 else [[b] for b in bits[2:]]
-    heads = [[[b] for b in bits[:2]], [[b] for b in bits[:2][::-1]]]
+    near = [[b] for b in bits[:2]]
+    far = [bits[2:4]] if k >= 4 else [[b] for b in bits[2:4]]
+    rest = [[b] for b in bits[4:]]
+
+    def order(p):
+        if p == n_item:
+            return far + near + rest
+        return (near if p % 2 == 0 else near[::-1]) + far + rest
 
     def plan(p):
         steps, off, rows, slot, sem = [], 0, PR, 0, 0
-        for group in [None] + heads[p % 2] + tail:
+        for group in [None] + order(p):
             ways = 2 if group is None else 1 << len(group)
             one = 1 if group is None else 1 << group[0]
             digit = grp if group is None else lax.rem(lax.div(dp, one), ways)
@@ -245,31 +252,40 @@
     outs = range(n_item, n_item + n_out)
     ins = range(n_item + n_out, parts)
 
+    reached = [0] * parts
+
+    def step(group):
+        for p in group:
+            if reached[p] < turns:
+                advance(p, reached[p])
+                reached[p] += 1
+
     for p in items:
         buf[p] = (SCALE * igrad[p * PR:(p + 1) * PR, :]).astype(BF16)
-        advance(p, 0)
+    step(items)
 
     g_out = dot(hidT[...], qgrad[...])
     for j, p in enumerate(outs):
         buf[p] = g_out[j * PR:(j + 1) * PR, :].astype(BF16)
-        advance(p, 0)
-    for p in items:
-        advance(p, 1)
+    step(outs)
+    step(items)
 
     for j, p in enumerate(ins):
         cols = slice(j * CW, (j + 1) * CW)
         hg = dot(qgrad[...], wqo[cols, :], NT)
         pg = (hg * slope[:, cols]).astype(BF16)
         buf[p] = dot(qfT[...], pg).astype(BF16)
-        advance(p, 0)
+        step([p])
+        if j == 0:
+            step(outs)
+        else:
+            step([p - 1])
         if j == 1:
-            for q in items:
-                advance(q, 2)
+            step(items)
 
     feat_wait()
     pf = to_pair(feats, 2)
     pf.start()
-    step_i = 3
 
     def item_back(j):
         cols = slice(j * CW, (j + 1) * CW)
@@ -284,19 +300,22 @@
         oii[:, cols] = dot(x, pg, TN) * factor
 
     done = 0
-    for n in range(1, turns):
-        for p in list(outs) + list(ins):
-            advance(p, n)
-        if step_i < turns:
-            for q in items:
-                advance(q, step_i)
-            step_i += 1
-            if step_i == turns:
+    landed = False
+    query = list(outs) + list(ins)
+    while min(reached) < turns:
+        before = max(reached[p] for p in items) < turns
+        step(items)
+        step(query[:len(query) // 2])
+        step(items)
+        step(query[len(query) // 2:])
+        if not before and done < n_in:
+            if not landed:
                 pf.wait()
-        elif done < n_in:
-            for _ in range(2):
-                item_back(done)
-                done += 1
+                landed = True
+            item_back(done)
+            done += 1
+    if not landed:
+        pf.wait()
     while done < n_in:
         item_back(done)
         done += 1
@@ -331,7 +350,7 @@
         parts = I // PR + H // PR + H // CW
         vm = pl.BlockSpec(memory_space=pltpu.VMEM)
         dma = pltpu.SemaphoreType.DMA
-        args = (qf, qw.reshape(1, Q), pos.reshape(1, Q), feat, ids.reshape(1, NI), logq.reshape(1, NI), wqi, wqo, wii, wio)
+        args = (qf, qw, pos.reshape(1, Q), feat, ids.reshape(1, NI), logq.reshape(1, NI), wqi, wqo, wii, wio)
         oqi, oqo, oii, oio, fac = pl.pallas_call(
             functools.partial(kernel, D, k, QT, AT, CW, PR),
             name="retrieval_grads",
@@ -345,7 +364,7 @@
             in_specs=[pl.BlockSpec(memory_space=pltpu.HBM)] * 10,
             out_specs=(vm,) * 5,
             scratch_shapes=[
-                pltpu.VMEM((Q, FE), BF16), pltpu.VMEM((1, Q), BF16), pltpu.VMEM((1, Q), jnp.int32),
+                pltpu.VMEM((Q, FE), BF16), pltpu.VMEM((Q,), BF16), pltpu.VMEM((1, Q), jnp.int32),
                 pltpu.VMEM((1, NI), jnp.int32), pltpu.VMEM((1, NI), BF16),
                 pltpu.VMEM((FE, H), BF16), pltpu.VMEM((H, E), BF16), pltpu.VMEM((FE, H), BF16), pltpu.VMEM((H, E), BF16),
                 dma((10,)),
@@ -358,6 +377,7 @@
                 pltpu.VMEM((FE, Q), BF16),
                 pltpu.VMEM((Q, E), BF16),
                 pltpu.VMEM((Q, E), BF16),
+                pltpu.VMEM((1, Q), F32),
                 pltpu.VMEM((I, E), F32),
                 pltpu.VMEM((parts, PR, E), BF16),
                 pltpu.VMEM((parts, PR + 64, E), BF16),

time: 63.4 us -> 65 us (1.025)
  Pallas kernels: 61.2 us -> 64.1 us
  local copies, waits for them, and re-layouts: 1.28 us -> 0 us
    pallas_call x1, Pallas kernels: 58.5 us -> 61.3 us  [on_device(): pl.pallas_call(functools.partial(kernel, D, k, QT, AT, CW, PR), name='ret...]
    reshape x1 -> x0, local copies, waits for them, and re-layouts: 1.28 us -> none  [on_device(): qw.reshape(1, Q)]
where the time goes in v3:
time: 65 us; the launch traced here: 64.7 us
  Pallas kernels  64.1 us (99%)
    pallas_call x1, Pallas kernels, on_device(): pl.pallas_call(functools.partial(kernel, D, k, QT, AT, CW, PR), name='ret...  61.3 us
    pallas_call x1, Pallas kernels, on_device(): pl.pallas_call(finish, name='finish', out_shape=(jax.ShapeDtypeStruct((FE...  2.74 us

profile of v3, /device:TPU:0, one launch (start us, length us, event | category | flops | bytes accessed | tf_op | source)
XLA Modules:
  0.0 64.7 jit_solution(12820926013144494882)
XLA Ops:
  0.6 61.3 %retrieval_grads.1 = (bf16[512,1024]{1,0:T(8,128)(2,1)S(1)}, bf16[1024,256]{1,0:T(8,128)(2,1)S(1)}, f32[512,1024]{1,0:T(8,128)S(1)}, f32[1024,256]{1,0:T(8,128)S(1)}, f32[8,128]{1,0:T(8,128)S(1)}) custom-call(bf16[1024,512]{1,0:T(8,128)(2,1)} %qf_h.1, bf16[1024]{0:T(1024)(128)(2,1)} %qw_h.1, s32[1,1024]{1,0:T(1,128)} %bitcast.3, bf16[16,512]{1,0:T(8,128)(2,1)} %feat_h.1, ...), custom_call_target="tpu_custom_call" | custom-call | tf_op jit(solution)/shard_map/retrieval_grads/pallas_call | solution.py:354
  62.0 2.7 %finish.1 = (f32[512,1024]{1,0:T(8,128)}, f32[1024,256]{1,0:T(8,128)}, f32[512,1024]{1,0:T(8,128)}, f32[1024,256]{1,0:T(8,128)}) custom-call(bf16[512,1024]{1,0:T(8,128)(2,1)S(1)} %get-tuple-element.9.qi, bf16[1024,256]{1,0:T(8,128)(2,1)S(1)} %get-tuple-element.10.qo, f32[512,1024]{1,0:T(8,128)S(1)} %get-tuple-element.11.ii, ...), custom_call_target="tpu_custom_call" | custom-call | tf_op jit(solution)/shard_map/finish/pallas_call | solution.py:392

commit v4 on v2

--- a/solution.py
+++ b/solution.py
@@ -30,7 +30,7 @@
     qf_h, qw_h, pos_h, feat_h, ids_h, logq_h, wqi_h, wqo_h, wii_h, wio_h,
     oqi, oqo, oii, oio, ofac,
     qf, qw, pos, ids, logq, wqi, wqo, wii, wio, load,
-    feats, meta, embs, slope, hid, hidT, qfT, qemb, qgrad, igrad, buf, rcv, gat,
+    feats, meta, embs, slope, hid, hidT, qfT, qemb, qgrad, wrow, igrad, buf, rcv, gat,
     em_send, em_recv, ag_send, ag_recv, mt_send, mt_recv, pair_send, pair_recv,
     rs_send, rs_recv, fg_send, fg_recv,
 ):
@@ -64,12 +64,13 @@
 
     for c in loads[:6]:
         c.wait()
+    wrow[...] = qw[...].astype(F32).reshape(1, Q)
     i_pre = dot(mine_at[...], wii[...])
     embs[dp, grp] = dot((i_pre * gate_of(i_pre)).astype(BF16), wio[...]).astype(BF16)
     meta[dp, grp] = jnp.zeros((8, 128), F32)
     meta[dp, grp, 0:1, 0:NI] = ids[...].astype(F32)
     meta[dp, grp, 1:2, 0:NI] = logq[...].astype(F32)
-    meta[dp, grp, 2:3, :] = jnp.broadcast_to(jnp.sum(qw[...].astype(F32), axis=1, keepdims=True), (1, 128))
+    meta[dp, grp, 2:3, :] = jnp.broadcast_to(jnp.sum(wrow[...], axis=1, keepdims=True), (1, 128))
 
     pl.semaphore_wait(barrier, D)
 
@@ -151,7 +152,7 @@
         m = jnp.maximum(jnp.max(s, axis=0, keepdims=True), -1e30)
         ex = jnp.exp(s - m)
         inv = 1.0 / jnp.sum(ex, axis=0, keepdims=True)
-        w = qw[:, rows].astype(F32)
+        w = wrow[:, rows]
         d = (w * (ex * inv - jnp.where(hit, 1.0, 0.0))).astype(BF16)
         term = dot(d, e_t)
         igrad[...] = jnp.where(t == 0, term, igrad[...] + term)
@@ -331,7 +332,7 @@
         parts = I // PR + H // PR + H // CW
         vm = pl.BlockSpec(memory_space=pltpu.VMEM)
         dma = pltpu.SemaphoreType.DMA
-        args = (qf, qw.reshape(1, Q), pos.reshape(1, Q), feat, ids.reshape(1, NI), logq.reshape(1, NI), wqi, wqo, wii, wio)
+        args = (qf, qw, pos.reshape(1, Q), feat, ids.reshape(1, NI), logq.reshape(1, NI), wqi, wqo, wii, wio)
         oqi, oqo, oii, oio, fac = pl.pallas_call(
             functools.partial(kernel, D, k, QT, AT, CW, PR),
             name="retrieval_grads",
@@ -345,7 +346,7 @@
             in_specs=[pl.BlockSpec(memory_space=pltpu.HBM)] * 10,
             out_specs=(vm,) * 5,
             scratch_shapes=[
-                pltpu.VMEM((Q, FE), BF16), pltpu.VMEM((1, Q), BF16), pltpu.VMEM((1, Q), jnp.int32),
+                pltpu.VMEM((Q, FE), BF16), pltpu.VMEM((Q,), BF16), pltpu.VMEM((1, Q), jnp.int32),
                 pltpu.VMEM((1, NI), jnp.int32), pltpu.VMEM((1, NI), BF16),
                 pltpu.VMEM((FE, H), BF16), pltpu.VMEM((H, E), BF16), pltpu.VMEM((FE, H), BF16), pltpu.VMEM((H, E), BF16),
                 dma((10,)),
@@ -358,6 +359,7 @@
                 pltpu.VMEM((FE, Q), BF16),
                 pltpu.VMEM((Q, E), BF16),
                 pltpu.VMEM((Q, E), BF16),
+                pltpu.VMEM((1, Q), F32),
                 pltpu.VMEM((I, E), F32),
                 pltpu.VMEM((parts, PR, E), BF16),
                 pltpu.VMEM((parts, PR + 64, E), BF16),

time: 63.4 us -> 62 us (0.978)
  local copies, waits for them, and re-layouts: 1.28 us -> 0 us
    reshape x1 -> x0, local copies, waits for them, and re-layouts: 1.28 us -> none  [on_device(): qw.reshape(1, Q)]
where the time goes in v4:
time: 62 us; the launch traced here: 61.7 us
  Pallas kernels  61.1 us (99%)
  between operations  0.64 us (1%)
    pallas_call x1, Pallas kernels, on_device(): pl.pallas_call(functools.partial(kernel, D, k, QT, AT, CW, PR), name='ret...  58.3 us
    pallas_call x1, Pallas kernels, on_device(): pl.pallas_call(finish, name='finish', out_shape=(jax.ShapeDtypeStruct((FE...  2.74 us

profile of v4, /device:TPU:0, one launch (start us, length us, event | category | flops | bytes accessed | tf_op | source)
XLA Modules:
  0.0 61.7 jit_solution(822074833516017920)
XLA Ops:
  0.6 58.3 %retrieval_grads.1 = (bf16[512,1024]{1,0:T(8,128)(2,1)S(1)}, bf16[1024,256]{1,0:T(8,128)(2,1)S(1)}, f32[512,1024]{1,0:T(8,128)S(1)}, f32[1024,256]{1,0:T(8,128)S(1)}, f32[8,128]{1,0:T(8,128)S(1)}) custom-call(bf16[1024,512]{1,0:T(8,128)(2,1)} %qf_h.1, bf16[1024]{0:T(1024)(128)(2,1)} %qw_h.1, s32[1,1024]{1,0:T(1,128)} %bitcast.3, bf16[16,512]{1,0:T(8,128)(2,1)} %feat_h.1, ...), custom_call_target="tpu_custom_call" | custom-call | tf_op jit(solution)/shard_map/retrieval_grads/pallas_call | solution.py:336
  59.0 2.7 %finish.1 = (f32[512,1024]{1,0:T(8,128)}, f32[1024,256]{1,0:T(8,128)}, f32[512,1024]{1,0:T(8,128)}, f32[1024,256]{1,0:T(8,128)}) custom-call(bf16[512,1024]{1,0:T(8,128)(2,1)S(1)} %get-tuple-element.9.qi, bf16[1024,256]{1,0:T(8,128)(2,1)S(1)} %get-tuple-element.10.qo, f32[512,1024]{1,0:T(8,128)S(1)} %get-tuple-element.11.ii, ...), custom_call_target="tpu_custom_call" | custom-call | tf_op jit(solution)/shard_map/finish/pallas_call | solution.py:374
